TPU v7x, 256 devices: a whole 4x4x8 slice. The times are simulated.
256 devices in a mesh: seq: 64 (over y, z, core), tp: 4 (over x).
Axes of the slice: x: 4, y: 4, z: 8, core: 2. Of those that a mesh axis runs over, the one named last changes fastest.
Arguments:
- stream: bfloat16 [8192, 2048], P('seq'), may hold values from -256 to 256
- lengths: int32 [6], replicated, may hold values from 1 to 7168, 8192 in all
- q_weight: bfloat16 [2048, 1536], P(None, 'tp'), may hold values from -0.125 to 0.125
- kv_down: bfloat16 [2048, 576], replicated, may hold values from -0.125 to 0.125
- latent_gain: float32 [512], replicated, may hold values from 0.1 to 1.9
- kv_up: bfloat16 [8, 512, 256], P('tp'), may hold values from -0.25 to 0.25
- out_weight: bfloat16 [1024, 2048], P('tp'), may hold values from -0.1875 to 0.1875
- moe_gain: float32 [2048], replicated, may hold values from 0.1 to 1.9
- routes: int32 [8192, 6], P('seq'), may hold values from 0 to 63, all different within a row; in each aligned block of 128 rows (0 to 127, 128 to 255, ...) at most 24 rows name the same one
- route_weight: float32 [8192, 6], P('seq'), may hold values from 0.05 to 0.5
- expert_gate: bfloat16 [64, 2048, 1408], P('seq', None, 'tp'), may hold values from -0.125 to 0.125
- expert_up: bfloat16 [64, 2048, 1408], P('seq', None, 'tp'), may hold values from -0.125 to 0.125
- expert_down: bfloat16 [64, 1408, 2048], P('seq', 'tp'), may hold values from -0.15625 to 0.15625
Outputs:
- layer_out: bfloat16 [8192, 2048], P('seq')
- latent_cache: bfloat16 [8192, 576], P('seq')
Inputs may be any that keep to these rules, and one draw needn't show every extreme that they name: 6 lengths summing to 8192, the longest exactly 7168. In each aligned block of 128 rows no expert is named by more than 24 routes, a bound that some block reaches.
All inputs are finite; a program needn't handle non-finite values.
Results may differ from a plain program's by a relative error of at most 0.0075.
Values may be sent and summed in bfloat16 or wider, within the bound.
A program may use at most 128 MiB of HBM per device.

v0:
```python
import jax
import jax.numpy as jnp
from jax import lax
from jax.sharding import PartitionSpec as P

D = 2048
NOPE = 128
ROPE = 64
LATENT = 512
VDIM = 128
THETA = 50000.0


def place(token_index, lengths):
    prompt_ends = jnp.cumsum(lengths)
    before = (prompt_ends[None, :] <= token_index[:, None]).astype(jnp.int32)
    segment = jnp.sum(before, axis=1)
    prompt_start = jnp.sum(before * lengths[None, :], axis=1)
    return (segment, token_index - prompt_start)


def angles(position):
    half_rope = ROPE // 2
    frequency = THETA ** (-2.0 * jnp.arange(half_rope, dtype=jnp.float32) / ROPE)
    angle_table = position.astype(jnp.float32)[:, None] * frequency[None, :]
    return (jnp.cos(angle_table), jnp.sin(angle_table))


def rotate(values, cos_table, sin_table):
    half_rope = ROPE // 2
    first_half = values[..., :half_rope]
    second = values[..., half_rope:]
    return jnp.concatenate(
        [first_half * cos_table - second * sin_table, first_half * sin_table + second * cos_table],
        axis=-1,
    )


def on_device(
    stream,
    lengths,
    q_weight,
    kv_down,
    latent_gain,
    kv_up,
    out_weight,
    moe_gain,
    routes,
    route_weight,
    expert_gate,
    expert_up,
    expert_down,
):
    tok_count = stream.shape[0]
    head_count = kv_up.shape[0]
    first_row = lax.axis_index("seq") * tok_count
    token_index = first_row + jnp.arange(tok_count, dtype=jnp.int32)
    segment, position = place(token_index, lengths)
    cos_table, sin_table = angles(position)
    kv_proj = jnp.dot(stream, kv_down, preferred_element_type=jnp.float32)
    compressed = kv_proj[:, :LATENT]
    factor = lax.rsqrt(jnp.mean(compressed * compressed, axis=1, keepdims=True) + 1e-06)
    latent = jnp.concatenate(
        [
            compressed * factor * latent_gain[None, :],
            rotate(kv_proj[:, LATENT:], cos_table, sin_table),
        ],
        axis=1,
    ).astype(jnp.bfloat16)
    q_proj = jnp.dot(stream, q_weight, preferred_element_type=jnp.float32).astype(jnp.bfloat16)
    q_proj = q_proj.reshape(tok_count, head_count, NOPE + ROPE)
    absorbed = jnp.einsum(
        "thj,hcj->thc", q_proj[:, :, :NOPE], kv_up[:, :, :NOPE], preferred_element_type=jnp.float32
    )
    rotated = rotate(
        q_proj[:, :, NOPE:].astype(jnp.float32), cos_table[:, None, :], sin_table[:, None, :]
    )
    softmax_scale = (NOPE + ROPE) ** (-0.5)
    queries = (jnp.concatenate([absorbed, rotated], axis=2) * softmax_scale).astype(jnp.bfloat16)
    queries = queries.reshape(tok_count * head_count, LATENT + ROPE)
    row_segment = jnp.repeat(segment, head_count)
    row_index = jnp.repeat(token_index, head_count)
    row_total = tok_count * head_count
    shard_rows = lax.all_gather(latent, "seq", axis=0, tiled=True)
    key_count = shard_rows.shape[0]
    key_index = jnp.arange(key_count, dtype=jnp.int32)
    key_segment, unused = place(key_index, lengths)
    allowed = (row_segment[:, None] == key_segment[None, :]) & (
        key_index[None, :] <= row_index[:, None]
    )
    running_max = jnp.full((row_total,), -1e30, jnp.float32)
    scores = jnp.einsum("ra,ka->rk", queries, shard_rows, preferred_element_type=jnp.float32)
    block_peak = jnp.max(jnp.where(allowed, scores, -jnp.inf), axis=1)
    new_peak = jnp.maximum(running_max, block_peak)
    weights = jnp.where(allowed, jnp.exp(scores - new_peak[:, None]), 0.0)
    running_sum = jnp.sum(weights, axis=1)
    context_sum = jnp.dot(
        weights.astype(jnp.bfloat16), shard_rows[:, :LATENT], preferred_element_type=jnp.float32
    )
    running_max, running_sum, context_sum = (new_peak, running_sum, context_sum)
    context = (context_sum / running_sum[:, None]).reshape(tok_count, head_count, LATENT)
    heads_out = jnp.einsum(
        "thc,hcv->thv",
        context,
        kv_up[:, :, NOPE:].astype(jnp.float32),
        precision=lax.Precision.HIGHEST,
    )
    heads_out = heads_out.astype(jnp.bfloat16).reshape(tok_count, head_count * VDIM)
    partial_attention = jnp.dot(heads_out, out_weight, preferred_element_type=jnp.float32)
    tp_count = lax.axis_size("tp")
    col_width = D // tp_count
    col_start = lax.axis_index("tp") * col_width
    attention_pieces = partial_attention.astype(jnp.bfloat16).reshape(
        tok_count, tp_count, col_width
    )
    attention_pieces = lax.all_to_all(
        attention_pieces.transpose(1, 0, 2), "tp", split_axis=0, concat_axis=0, tiled=True
    )
    attention_part = jnp.sum(attention_pieces.astype(jnp.float32), axis=0)
    stream_part = lax.dynamic_slice_in_dim(stream, col_start, col_width, 1)
    hidden = stream_part.astype(jnp.float32) + attention_part
    normed = hidden.astype(jnp.bfloat16)
    experts = lax.axis_size("seq")
    top_k = routes.shape[1]
    capacity = min(tok_count, max(2, 2 * tok_count * top_k // experts))
    flat_routes = routes.reshape(-1)
    onehot = (flat_routes[:, None] == jnp.arange(experts, dtype=jnp.int32)[None, :]).astype(
        jnp.int32
    )
    slot_rank = jnp.sum((jnp.cumsum(onehot, axis=0) - onehot) * onehot, axis=1)
    slot_index = flat_routes * capacity + slot_rank
    slot_table = (
        slot_index[:, None] == jnp.arange(experts * capacity, dtype=jnp.int32)[None, :]
    ).astype(jnp.bfloat16)
    placing = jnp.sum(slot_table.reshape(tok_count, top_k, experts * capacity), axis=1)
    outgoing = jnp.einsum("ts,td->sd", placing, normed, preferred_element_type=jnp.float32).astype(
        jnp.bfloat16
    )
    outgoing = outgoing.reshape(experts, capacity, col_width)
    chunk_count = 2
    chunk_slots = capacity // chunk_count
    returned_chunks = []
    for chunk in range(chunk_count):
        sending = outgoing[:, chunk * chunk_slots : (chunk + 1) * chunk_slots]
        received = lax.all_to_all(sending, "seq", split_axis=0, concat_axis=0, tiled=True)
        sources, slot_count, _ = received.shape
        flat_part = received.reshape(sources * slot_count, col_width)
        flat_rows = lax.all_gather(flat_part, "tp", axis=1, tiled=True).astype(jnp.float32)
        flat_rows = (
            flat_rows
            * lax.rsqrt(jnp.mean(flat_rows * flat_rows, axis=1, keepdims=True) + 1e-06)
            * moe_gain[None, :]
        ).astype(jnp.bfloat16)
        gate_act = jnp.dot(flat_rows, expert_gate[0], preferred_element_type=jnp.float32)
        up_act = jnp.dot(flat_rows, expert_up[0], preferred_element_type=jnp.float32)
        hidden_units = (jax.nn.silu(gate_act) * up_act).astype(jnp.bfloat16)
        expert_out = jnp.dot(
            hidden_units, expert_down[0], preferred_element_type=jnp.float32
        ).astype(jnp.bfloat16)
        expert_sum = lax.psum_scatter(expert_out, "tp", scatter_dimension=1, tiled=True)
        expert_sum = expert_sum.reshape(sources, slot_count, col_width)
        returned_chunks.append(
            lax.all_to_all(expert_sum, "seq", split_axis=0, concat_axis=0, tiled=True)
        )
    returned = jnp.concatenate(returned_chunks, axis=1)
    gathered = returned.reshape(experts * capacity, col_width)[slot_index].reshape(
        tok_count, top_k, col_width
    )
    moe = jnp.zeros((tok_count, col_width), jnp.float32)
    for route_slot in range(top_k):
        moe = moe + route_weight[:, route_slot][:, None] * gathered[:, route_slot].astype(
            jnp.float32
        )
    layer_part = (hidden + moe).astype(jnp.bfloat16)
    repeated_part = jnp.broadcast_to(layer_part[None], (tp_count,) + layer_part.shape)
    layer_pieces = lax.all_to_all(repeated_part, "tp", split_axis=0, concat_axis=0, tiled=True)
    layer_out = layer_pieces.transpose(1, 0, 2).reshape(tok_count, D)
    return (layer_out, latent)


def solution(mesh):
    return jax.shard_map(
        on_device,
        mesh=mesh,
        in_specs=(
            P("seq", None),
            P(),
            P(None, "tp"),
            P(),
            P(),
            P("tp", None, None),
            P("tp", None),
            P(),
            P("seq", None),
            P("seq", None),
            P("seq", None, "tp"),
            P("seq", None, "tp"),
            P("seq", "tp", None),
        ),
        out_specs=(P("seq", None), P("seq", None)),
        check_vma=False,
    )
```

profile of v0, /device:TPU:1, one launch (start us, length us, event | category | flops | bytes accessed | tf_op | source)
XLA Modules:
  0.0 411.8 jit_solution(14239379274214092569)
XLA Ops:
  7.3 1.0 reduce-window.18
  8.3 0.7 fusion.82
  9.1 1.9 fusion.94
  11.0 0.1 multiply_cosine_fusion
  11.2 0.1 multiply_convert_fusion
  11.3 0.7 pad_maximum_fusion.1
  12.2 0.1 eq.62
  12.3 0.1 eq.58
  12.4 1.8 convolution_convert_fusion.4
  14.3 0.1 copy.93
  14.4 0.1 copy.96
  14.6 0.1 copy.97
  14.8 0.2 eq.54
  15.0 0.2 le.48
  15.2 0.3 convolution_bitcast_fusion
  15.4 0.4 copy.95
  15.8 0.4 concatenate.17
  16.2 1.8 reduce-window.19
  18.0 0.3 slice_reduce_fusion
  18.3 0.1 fusion.76
  18.5 0.1 reduce_sum.104
  18.6 0.2 convert_reduce_fusion.1
  18.8 84.7 %all-gather.4.cloned.1.call-done = bf16[8192,576]{0,1:T(8,128)(2,1)} async-done(((bf16[128,576]{0,1:T(8,128)(2,1)}), bf16[8192,576]{0,1:T(8,128)(2,1)}) %all-gather.4.cloned.1.call-update) | async-done | bytes 9437200 | tf_op jit(solution)/shard_map/all_gather | solution.py:84
  103.5 6.8 %select_reduce_fusion = (f32[256]{0:T(256)S(1)}, f32[256,8192]{1,0:T(8,128)S(1)}) fusion(s32[256]{0:T(256)S(1)} %le.48, s32[8192]{0:T(1024)S(1)} %convert_reduce_fusion.1, s32[256]{0:T(256)S(1)} %eq.54, bf16[8192,576]{0,1:T(8,128)(2,1)} %all-gather.4.cloned.1.call-done, f32[256,32]{1,0:T(8,128)S(1)} %bitcast.130, f32[256,32]{1,0:T(8,128)S(1)} %bitcast.129, ...), kind=kOutput, calls=%fused_computation.4 | convolution fusion | flops 2426994432 | bytes 18451456 | tf_op jit(solution)/shard_map/ra,ka->rk/dot_general | solution.py:92
  110.3 2.8 fusion.9
  113.1 6.3 %fusion.41 = f32[256,512]{1,0:T(8,128)S(1)} fusion(bf16[8192,576]{0,1:T(8,128)(2,1)} %all-gather.4.cloned.1.call-done, f32[256,8192]{1,0:T(8,128)S(1)} %get-tuple-element.33, f32[256]{0:T(256)S(1)} %broadcast_maximum_fusion, s32[256]{0:T(256)S(1)} %le.48, s32[8192]{0:T(1024)S(1)} %convert_reduce_fusion.1, s32[256]{0:T(256)S(1)} %eq.54, f32[256]{0:T(256)S(1)} %fusion.9), kind=kOutput, calls=%fused_computation.49 | convolution fusion | flops 2160197632 | bytes 17338368 | tf_op jit(solution)/shard_map/dot_general | solution.py:97
  119.5 0.3 reshape.240
  119.8 0.5 convolution_convert_fusion.5
  120.3 0.3 convolution_convert_fusion.3
  120.6 0.8 copy.143
  121.5 4.0 all-to-all-start
  125.5 0.7 fusion.18
  126.2 8.2 %all-to-all-done = bf16[4,128,512]{2,1,0:T(8,128)(2,1)S(1)} async-done(((bf16[4,128,512]{2,1,0:T(8,128)(2,1)}), bf16[4,128,512]{2,1,0:T(8,128)(2,1)S(1)}, u32[]{:S(2)}, u32[]{:S(2)}) %all-to-all-start) | async-done | bytes 524320 | tf_op jit(solution)/shard_map/all_to_all | solution.py:116
  134.5 0.6 convolution_convert_fusion.2
  135.2 0.5 fusion.92
  135.7 39.2 %all_to_all.30 = bf16[64,12,512]{2,1,0:T(8,128)(2,1)S(1)} all-to-all(bf16[64,12,512]{2,1,0:T(8,128)(2,1)S(1)} %get-tuple-element.8), channel_id=1, replica_groups=mesh['seq'=64,'tp'=4] {'seq'}, dimensions={0} | all-to-all | bytes 1572864 | tf_op jit(solution)/shard_map/all_to_all | solution.py:145
  174.9 1.1 reshape.245
  176.0 34.5 %all_to_all.31 = bf16[64,12,512]{2,1,0:T(8,128)(2,1)S(1)} all-to-all(bf16[64,12,512]{2,1,0:T(8,128)(2,1)S(1)} %get-tuple-element.9), channel_id=1, replica_groups=mesh['seq'=64,'tp'=4] {'seq'}, dimensions={0} | all-to-all | bytes 1572864 | tf_op jit(solution)/shard_map/all_to_all | solution.py:145
  210.6 1.1 reshape.247
  211.8 1.2 all-gather.6.cloned.1.call-done
  213.0 2.7 fusion.3
  215.8 3.8 fusion.27
  219.6 7.6 %convolution_convert_fusion.1 = bf16[768,2048]{1,0:T(8,128)(2,1)} fusion(bf16[1,352,2048]{2,1,0:T(8,128)(2,1)} %param.25, bf16[1,2048,352]{1,2,0:T(8,128)(2,1)} %param.24, f32[768,352]{0,1:T(8,128)} %fusion.27, bf16[768,2048]{1,0:T(8,128)(2,1)S(1)} %copy-done.4, f32[2048]{0:T(1024)S(1)} %copy-done.12, f32[768]{0:T(1024)S(1)} %add_rsqrt_fusion.1), kind=kOutput, calls=%fused_computation.27 | convolution fusion | flops 2224078848 | bytes 10267648 | tf_op jit(solution)/shard_map/dot_general | solution.py:157
  227.2 0.3 reduce-scatter.5.cloned.1.call-start
  227.5 29.6 %all-gather.8.cloned.1.call-done = bf16[768,2048]{1,0:T(8,128)(2,1)} async-done(((bf16[768,512]{1,0:T(8,128)(2,1)}), bf16[768,2048]{1,0:T(8,128)(2,1)}) %all-gather.8.cloned.1.call-update) | async-done | bytes 3145744 | tf_op jit(solution)/shard_map/all_gather | solution.py:148
  257.1 2.7 fusion.6
  259.9 3.8 fusion.25
  263.7 7.6 %convolution_convert_fusion = bf16[768,2048]{1,0:T(8,128)(2,1)} fusion(bf16[1,352,2048]{2,1,0:T(8,128)(2,1)} %param.25, bf16[1,2048,352]{1,2,0:T(8,128)(2,1)} %param.24, f32[768,352]{0,1:T(8,128)} %fusion.25, bf16[768,2048]{1,0:T(8,128)(2,1)S(1)} %copy-done.3, f32[768]{0:T(1024)S(1)} %add_rsqrt_fusion, f32[2048]{0:T(1024)S(1)} %copy-done.12), kind=kOutput, calls=%fused_computation.26 | convolution fusion | flops 2224078848 | bytes 10267648 | tf_op jit(solution)/shard_map/dot_general | solution.py:157
  271.3 29.3 %reduce-scatter.3.cloned.1.call-done = bf16[768,512]{1,0:T(8,128)(2,1)} async-done(((bf16[768,2048]{1,0:T(8,128)(2,1)}), bf16[768,512]{1,0:T(8,128)(2,1)}) %reduce-scatter.3.cloned.1.call-update) | async-done | bytes 786448 | tf_op jit(solution)/shard_map/reduce_scatter | solution.py:160
  300.6 2.1 reshape.246
  302.8 10.9 %all-to-all-start.2 = ((bf16[64,12,512]{2,1,0:T(8,128)(2,1)}), bf16[64,12,512]{2,1,0:T(8,128)(2,1)S(1)}, u32[]{:S(2)}, u32[]{:S(2)}) async-start(bf16[64,12,512]{2,1,0:T(8,128)(2,1)} %reshape.246), calls=%async_computation.3 | async-start | bytes 2097152 | tf_op jit(solution)/shard_map/all_to_all | solution.py:163
  313.6 30.0 %reduce-scatter.5.cloned.1.call-done = bf16[768,512]{1,0:T(8,128)(2,1)} async-done(((bf16[768,2048]{1,0:T(8,128)(2,1)}), bf16[768,512]{1,0:T(8,128)(2,1)}) %reduce-scatter.5.cloned.1.call-update) | async-done | bytes 786448 | tf_op jit(solution)/shard_map/reduce_scatter | solution.py:160
  343.7 2.2 reshape.248
  345.8 10.9 %all-to-all-start.4 = ((bf16[64,12,512]{2,1,0:T(8,128)(2,1)}), bf16[64,12,512]{2,1,0:T(8,128)(2,1)}, u32[]{:S(2)}, u32[]{:S(2)}) async-start(bf16[64,12,512]{2,1,0:T(8,128)(2,1)} %reshape.248), calls=%async_computation.6 | async-start | bytes 2097152 | tf_op jit(solution)/shard_map/all_to_all | solution.py:163
  356.8 0.1 mul.276
  357.0 28.2 %all-to-all-done.4 = bf16[64,12,512]{2,1,0:T(8,128)(2,1)} async-done(((bf16[64,12,512]{2,1,0:T(8,128)(2,1)}), bf16[64,12,512]{2,1,0:T(8,128)(2,1)}, u32[]{:S(2)}, u32[]{:S(2)}) %all-to-all-start.4) | async-done | bytes 786464 | tf_op jit(solution)/shard_map/all_to_all | solution.py:163
  385.2 1.7 pad_maximum_fusion
  386.9 2.7 gather_fusion
  389.6 0.3 reshape.250
  389.9 1.1 fusion.93
  391.0 1.1 fusion.67
  392.2 11.7 %all_to_all.32 = bf16[4,128,512]{2,1,0:T(8,128)(2,1)S(1)} all-to-all(bf16[4,128,512]{2,1,0:T(8,128)(2,1)S(1)} %broadcast_in_dim.20), channel_id=1, replica_groups=mesh['seq'=64,'tp'=4] {'tp'}, dimensions={0} | all-to-all | bytes 1048576 | tf_op jit(solution)/shard_map/all_to_all | solution.py:176
  403.9 0.3 copy.111
  404.2 1.0 copy.112
  (58 shorter events, 1.2 us)
Async XLA Ops:
  7.2 1.9 copy-start
  7.2 5.2 %copy-start.2 = (bf16[128,2048]{1,0:T(8,128)(2,1)S(1)}, bf16[128,2048]{1,0:T(8,128)(2,1)}, u32[]{:S(2)}) copy-start(bf16[128,2048]{1,0:T(8,128)(2,1)} %param.13) | copy-start | bytes 1572868
  7.2 4.0 copy-start.11
  7.2 4.8 %copy-start.9 = (s32[128,6]{0,1:T(8,128)S(1)}, s32[128,6]{0,1:T(8,128)}, u32[]{:S(2)}) copy-start(s32[128,6]{0,1:T(8,128)} %param.21) | copy-start | bytes 9220
  7.2 96.3 %all-gather.4.cloned.1.call-start = ((), (), s32[]{:S(2)}) async-start(), calls=%async_computation.8 | async-start | bytes 9584640 | tf_op jit(solution)/shard_map/all_gather | solution.py:84
  9.0 6.1 %copy-start.8 = (bf16[2,512,256]{2,1,0:T(8,128)(2,1)S(1)}, bf16[2,512,256]{2,1,0:T(8,128)(2,1)}, u32[]{:S(2)}) copy-start(bf16[2,512,256]{2,1,0:T(8,128)(2,1)} %param.18) | copy-start | bytes 1572868
  113.1 7.2 %copy-start.7 = (bf16[256,2048]{1,0:T(8,128)(2,1)S(1)}, bf16[256,2048]{1,0:T(8,128)(2,1)}, u32[]{:S(2)}) copy-start(bf16[256,2048]{1,0:T(8,128)(2,1)} %param.19) | copy-start | bytes 3145732
  121.5 13.0 %all-to-all-start = ((bf16[4,128,512]{2,1,0:T(8,128)(2,1)}), bf16[4,128,512]{2,1,0:T(8,128)(2,1)S(1)}, u32[]{:S(2)}, u32[]{:S(2)}) async-start(bf16[4,128,512]{2,1,0:T(8,128)(2,1)} %bitcast.120), calls=%async_computation | async-start | bytes 1048576 | tf_op jit(solution)/shard_map/all_to_all | solution.py:116
  125.4 87.6 %all-gather.6.cloned.1.call-start = ((), (), s32[]{:S(2)}) async-start(), calls=%async_computation.9 | async-start | bytes 3932160 | tf_op jit(solution)/shard_map/all_gather | solution.py:148
  134.5 0.7 copy-start.5
  176.0 81.1 %all-gather.8.cloned.1.call-start = ((), (), s32[]{:S(2)}) async-start(), calls=%async_computation.11 | async-start | bytes 3932160 | tf_op jit(solution)/shard_map/all_gather | solution.py:148
  210.6 5.2 %copy-start.12 = (f32[2048]{0:T(1024)S(1)}, f32[2048]{0:T(1024)}, u32[]{:S(2)}) copy-start(f32[2048]{0:T(1024)} %param.20) | copy-start | bytes 24580
  211.7 88.9 %reduce-scatter.3.cloned.1.call-start = ((), (), s32[]{:S(2)}) async-start(), calls=%async_computation.10 | async-start | bytes 3932160 | tf_op jit(solution)/shard_map/reduce_scatter | solution.py:160
  213.0 2.8 copy-start.4
  227.2 116.4 %reduce-scatter.5.cloned.1.call-start = ((), (), s32[]{:S(2)}) async-start(), calls=%async_computation.12 | async-start | bytes 3932160 | tf_op jit(solution)/shard_map/reduce_scatter | solution.py:160
  257.1 2.8 copy-start.3
  302.8 54.2 %copy-start.10 = (f32[128,6]{0,1:T(8,128)S(1)}, f32[128,6]{0,1:T(8,128)}, u32[]{:S(2)}) copy-start(f32[128,6]{0,1:T(8,128)} %param.22) | copy-start | bytes 9220
  302.8 43.1 %all-to-all-start.2 = ((bf16[64,12,512]{2,1,0:T(8,128)(2,1)}), bf16[64,12,512]{2,1,0:T(8,128)(2,1)S(1)}, u32[]{:S(2)}, u32[]{:S(2)}) async-start(bf16[64,12,512]{2,1,0:T(8,128)(2,1)} %reshape.246), calls=%async_computation.3 | async-start | bytes 2097152 | tf_op jit(solution)/shard_map/all_to_all | solution.py:163
  345.8 39.4 %all-to-all-start.4 = ((bf16[64,12,512]{2,1,0:T(8,128)(2,1)}), bf16[64,12,512]{2,1,0:T(8,128)(2,1)}, u32[]{:S(2)}, u32[]{:S(2)}) async-start(bf16[64,12,512]{2,1,0:T(8,128)(2,1)} %reshape.248), calls=%async_computation.6 | async-start | bytes 2097152 | tf_op jit(solution)/shard_map/all_to_all | solution.py:163
  389.9 1.2 copy-start.6
  389.9 15.3 %copy-start.1 = (bf16[2048,576]{0,1:T(8,128)(2,1)S(1)}, bf16[2048,576]{0,1:T(8,128)(2,1)}, u32[]{:S(2)}) copy-start(bf16[2048,576]{0,1:T(8,128)(2,1)} %param.16) | copy-start | bytes 7077892
Sparse Core Ops, SparseCore 0:
  12.1 91.3 all-gather.3
  176.1 36.8 all-gather.5
  214.8 42.2 all-gather.7
  259.5 41.1 reduce-scatter.2
  303.0 40.5 reduce-scatter.4
where the time goes:
time: 412 us
  waiting for transfers between devices  211 us (51%)
  blocking collectives  85.4 us (21%)
  matrix products  41.3 us (10%)
  starting transfers between devices  26.2 us (6%)
  other arithmetic  18 us (4%)
  local copies, waits for them, and re-layouts  15.3 us (4%)
  between operations  14.2 us (3%)
    all_gather x1, waiting for transfers between devices, on_device(): shard_rows = lax.all_gather(latent, 'seq', axis=0, tiled=True)  84.7 us
    all_to_all x2, blocking collectives, on_device(): lax.all_to_all(sending, 'seq', split_axis=0, concat_axis=0, tiled=True)  73.7 us
    reduce_scatter x2, waiting for transfers between devices, on_device(): lax.psum_scatter(expert_out, 'tp', scatter_dimension=1, tiled=True)  59.3 us
    all_gather x2, waiting for transfers between devices, on_device(): lax.all_gather(flat_part, 'tp', axis=1, tiled=True).astype(jnp.float32)  30.8 us
    all_to_all x2, waiting for transfers between devices, on_device(): lax.all_to_all(expert_sum, 'seq', split_axis=0, concat_axis=0, tiled=True)  28.2 us
    all_to_all x2, starting transfers between devices, on_device(): lax.all_to_all(expert_sum, 'seq', split_axis=0, concat_axis=0, tiled=True)  21.8 us
    dot_general x2, matrix products, on_device(): jnp.dot(hidden_units, expert_down[0], preferred_element_type=jnp.float32)  15.2 us
    all_to_all x1, blocking collectives, on_device(): lax.all_to_all(repeated_part, 'tp', split_axis=0, concat_axis=0, tiled=True)  11.7 us
  transfers between devices with their start and end apart: 8, of which 7 were waited for; matrix products, arithmetic and copies ran while one was open for 10% of the time, Pallas kernels for 0%

commit v1 on v0

--- a/solution.py
+++ b/solution.py
@@ -2,6 +2,7 @@
 import jax.numpy as jnp
 from jax import lax
 from jax.sharding import PartitionSpec as P
+from jax.lax import all_to_all, axis_size
 
 D = 2048
 NOPE = 128
@@ -81,7 +82,13 @@
     row_segment = jnp.repeat(segment, head_count)
     row_index = jnp.repeat(token_index, head_count)
     row_total = tok_count * head_count
-    shard_rows = lax.all_gather(latent, "seq", axis=0, tiled=True)
+    total_devices = axis_size("seq")
+    lanes = []
+    s = 0
+    while s < latent.ndim:
+        lanes.append(total_devices if s == 0 else 1)
+        s = s + 1
+    shard_rows = all_to_all(jnp.tile(latent, lanes), "seq", split_axis=0, concat_axis=0, tiled=True)
     key_count = shard_rows.shape[0]
     key_index = jnp.arange(key_count, dtype=jnp.int32)
     key_segment, unused = place(key_index, lengths)

time: 412 us -> 558 us (1.35)
  waiting for transfers between devices: 211 us -> 330 us
  local copies, waits for them, and re-layouts: 15.3 us -> 33.1 us
  starting transfers between devices: 26.2 us -> 39.7 us
    all_to_all x0 -> x1, waiting for transfers between devices: none -> 203 us  [on_device(): all_to_all(jnp.tile(latent, lanes), 'seq', split_axis=0, concat_axis=0, t...]
    all_gather x1 -> x0, waiting for transfers between devices: 84.7 us -> none  [on_device(): shard_rows = lax.all_gather(latent, 'seq', axis=0, tiled=True)]
    all_to_all x0 -> x1, starting transfers between devices: none -> 13.5 us  [on_device(): all_to_all(jnp.tile(latent, lanes), 'seq', split_axis=0, concat_axis=0, t...]
    all_to_all x0 -> x1, local copies, waits for them, and re-layouts: none -> 8.73 us  [on_device(): all_to_all(jnp.tile(latent, lanes), 'seq', split_axis=0, concat_axis=0, t...]
    another operation x0 -> x1, local copies, waits for them, and re-layouts: none -> 5.93 us  [on_device(): jnp.tile(latent, lanes)]
  transfers between devices with their start and end apart: 8 -> 8, of which waited for: 7 -> 7; matrix products, arithmetic and copies ran while one was open for 10% -> 7% of each run, Pallas kernels for 0% -> 0%
where the time goes in v1:
time: 558 us; the launch traced here: 557 us
  waiting for transfers between devices  330 us (59%)
  blocking collectives  80.1 us (14%)
  matrix products  42 us (8%)
  starting transfers between devices  39.7 us (7%)
  local copies, waits for them, and re-layouts  33.1 us (6%)
  other arithmetic  17.3 us (3%)
  between operations  14.3 us (3%)
    all_to_all x1, waiting for transfers between devices, on_device(): all_to_all(jnp.tile(latent, lanes), 'seq', split_axis=0, concat_axis=0, t...  203 us
    all_to_all x2, blocking collectives, on_device(): lax.all_to_all(sending, 'seq', split_axis=0, concat_axis=0, tiled=True)  68.4 us
    reduce_scatter x2, waiting for transfers between devices, on_device(): lax.psum_scatter(expert_out, 'tp', scatter_dimension=1, tiled=True)  59.9 us
    all_gather x2, waiting for transfers between devices, on_device(): lax.all_gather(flat_part, 'tp', axis=1, tiled=True).astype(jnp.float32)  30.2 us
    all_to_all x2, waiting for transfers between devices, on_device(): lax.all_to_all(expert_sum, 'seq', split_axis=0, concat_axis=0, tiled=True)  28.2 us
    all_to_all x2, starting transfers between devices, on_device(): lax.all_to_all(expert_sum, 'seq', split_axis=0, concat_axis=0, tiled=True)  21.8 us
    dot_general x2, matrix products, on_device(): jnp.dot(hidden_units, expert_down[0], preferred_element_type=jnp.float32)  16.7 us
    all_to_all x1, starting transfers between devices, on_device(): all_to_all(jnp.tile(latent, lanes), 'seq', split_axis=0, concat_axis=0, t...  13.5 us
  transfers between devices with their start and end apart: 8, of which 7 were waited for; matrix products, arithmetic and copies ran while one was open for 7% of the time, Pallas kernels for 0%

profile of v1, /device:TPU:1, one launch (start us, length us, event | category | flops | bytes accessed | tf_op | source)
XLA Modules:
  0.0 556.8 jit_solution(14363406447608806796)
XLA Ops:
  7.2 1.0 reduce-window.18
  8.2 0.7 fusion.82
  9.0 1.8 fusion.94
  10.9 0.1 multiply_cosine_fusion
  11.1 0.1 multiply_convert_fusion
  11.2 5.9 %tile.2 = bf16[64,128,576]{1,2,0:T(8,128)(2,1)} broadcast(bf16[128,576]{0,1:T(8,128)(2,1)S(1)} %pad_maximum_fusion.1), dimensions={1,2} | broadcast | bytes 9584640 | tf_op jit(solution)/shard_map/tile | solution.py:91
  17.2 13.5 %all-to-all-start = ((bf16[64,128,576]{1,2,0:T(8,128)(2,1)}), bf16[64,128,576]{1,2,0:T(8,128)(2,1)}, u32[]{:S(2)}, u32[]{:S(2)}) async-start(bf16[64,128,576]{1,2,0:T(8,128)(2,1)} %tile.2), calls=%async_computation | async-start | bytes 18874368 | tf_op jit(solution)/shard_map/all_to_all | solution.py:91
  30.8 0.1 eq.62
  30.9 0.1 eq.58
  31.1 0.4 convolution_convert_fusion.4
  32.0 0.2 eq.54
  32.2 0.2 le.48
  32.4 0.3 convolution_bitcast_fusion
  32.6 0.4 copy.99
  33.1 0.4 concatenate.21
  33.5 1.8 reduce-window.19
  35.3 0.3 slice_reduce_fusion
  35.6 0.1 fusion.76
  35.7 0.1 reduce_sum.104
  35.8 0.2 convert_reduce_fusion.1
  36.0 202.9 %all-to-all-done = bf16[64,128,576]{1,2,0:T(8,128)(2,1)} async-done(((bf16[64,128,576]{1,2,0:T(8,128)(2,1)}), bf16[64,128,576]{1,2,0:T(8,128)(2,1)}, u32[]{:S(2)}, u32[]{:S(2)}) %all-to-all-start) | async-done | bytes 9437216 | tf_op jit(solution)/shard_map/all_to_all | solution.py:91
  238.9 6.7 %select_reduce_fusion = (f32[256]{0:T(256)S(1)}, f32[256,8192]{1,0:T(8,128)S(1)}) fusion(s32[256]{0:T(256)S(1)} %le.48, s32[8192]{0:T(1024)S(1)} %convert_reduce_fusion.1, s32[256]{0:T(256)S(1)} %eq.54, f32[256,32]{1,0:T(8,128)S(1)} %bitcast.140, f32[256,32]{1,0:T(8,128)S(1)} %bitcast.139, f32[256,512]{1,0:T(8,128)S(1)} %concatenate.21, ...), kind=kOutput, calls=%fused_computation.5 | convolution fusion | flops 2426994432 | bytes 18451456 | tf_op jit(solution)/shard_map/ra,ka->rk/dot_general | solution.py:99
  245.6 3.3 copy-done.2
  248.9 2.7 fusion.9
  251.7 8.7 %copy_bitcast_fusion = bf16[8192,576]{0,1:T(8,128)(2,1)} fusion(bf16[64,128,576]{1,2,0:T(8,128)(2,1)} %all-to-all-done), kind=kLoop, calls=%fused_computation.1 | loop fusion | bytes 18874368 | tf_op jit(solution)/shard_map/all_to_all | solution.py:91
  260.4 8.4 %fusion.41 = f32[256,512]{1,0:T(8,128)S(1)} fusion(bf16[8192,576]{0,1:T(8,128)(2,1)} %copy_bitcast_fusion, f32[256,8192]{1,0:T(8,128)} %copy-done.2, f32[256]{0:T(256)S(1)} %broadcast_maximum_fusion, s32[256]{0:T(256)S(1)} %le.48, s32[8192]{0:T(1024)S(1)} %convert_reduce_fusion.1, s32[256]{0:T(256)S(1)} %eq.54, f32[256]{0:T(256)S(1)} %fusion.9), kind=kOutput, calls=%fused_computation.50 | convolution fusion | flops 2160197632 | bytes 17338368 | tf_op jit(solution)/shard_map/dot_general | solution.py:104
  268.8 0.3 reshape.268
  269.1 0.5 convolution_convert_fusion.5
  269.6 0.3 convolution_convert_fusion.3
  269.9 0.8 copy.153
  270.8 4.0 all-to-all-start.1
  274.9 0.7 fusion.18
  275.6 9.1 %all-to-all-done.1 = bf16[4,128,512]{2,1,0:T(8,128)(2,1)S(1)} async-done(((bf16[4,128,512]{2,1,0:T(8,128)(2,1)}), bf16[4,128,512]{2,1,0:T(8,128)(2,1)S(1)}, u32[]{:S(2)}, u32[]{:S(2)}) %all-to-all-start.1) | async-done | bytes 524320 | tf_op jit(solution)/shard_map/all_to_all | solution.py:123
  284.8 0.6 convolution_convert_fusion.2
  285.4 0.5 fusion.92
  285.8 33.9 %all_to_all.39 = bf16[64,12,512]{2,1,0:T(8,128)(2,1)S(1)} all-to-all(bf16[64,12,512]{2,1,0:T(8,128)(2,1)S(1)} %get-tuple-element.8), channel_id=1, replica_groups=mesh['seq'=64,'tp'=4] {'seq'}, dimensions={0} | all-to-all | bytes 1572864 | tf_op jit(solution)/shard_map/all_to_all | solution.py:152
  319.8 1.1 reshape.273
  320.9 34.5 %all_to_all.40 = bf16[64,12,512]{2,1,0:T(8,128)(2,1)S(1)} all-to-all(bf16[64,12,512]{2,1,0:T(8,128)(2,1)S(1)} %get-tuple-element.9), channel_id=1, replica_groups=mesh['seq'=64,'tp'=4] {'seq'}, dimensions={0} | all-to-all | bytes 1572864 | tf_op jit(solution)/shard_map/all_to_all | solution.py:152
  355.4 1.0 reshape.275
  356.5 1.3 all-gather.3.cloned.1.call-done
  357.8 2.7 fusion.3
  360.7 3.9 fusion.27
  364.6 8.1 %convolution_convert_fusion.1 = bf16[768,2048]{1,0:T(8,128)(2,1)} fusion(bf16[1,352,2048]{2,1,0:T(8,128)(2,1)S(1)} %copy-done.16, bf16[1,2048,352]{1,2,0:T(8,128)(2,1)} %param.24, f32[768,352]{0,1:T(8,128)} %fusion.27, bf16[768,2048]{1,0:T(8,128)(2,1)} %all-gather.3.cloned.1.call-done, f32[2048]{0:T(1024)S(1)} %copy-done.17, f32[768]{0:T(1024)S(1)} %add_rsqrt_fusion.1), kind=kOutput, calls=%fused_computation.28 | convolution fusion | flops 2224078848 | bytes 10267648 | tf_op jit(solution)/shard_map/dot_general | solution.py:164
  372.7 0.3 reduce-scatter.5.cloned.1.call-start
  373.0 28.9 %all-gather.5.cloned.1.call-done = bf16[768,2048]{1,0:T(8,128)(2,1)} async-done(((bf16[768,512]{1,0:T(8,128)(2,1)}), bf16[768,2048]{1,0:T(8,128)(2,1)}) %all-gather.5.cloned.1.call-update) | async-done | bytes 3145744 | tf_op jit(solution)/shard_map/all_gather | solution.py:155
  401.9 2.7 fusion.6
  404.7 2.4 fusion.25
  407.1 8.6 %convolution_convert_fusion = bf16[768,2048]{1,0:T(8,128)(2,1)} fusion(bf16[1,352,2048]{2,1,0:T(8,128)(2,1)} %param.25, bf16[1,2048,352]{1,2,0:T(8,128)(2,1)} %param.24, f32[768,352]{0,1:T(8,128)} %fusion.25, bf16[768,2048]{1,0:T(8,128)(2,1)} %all-gather.5.cloned.1.call-done, f32[768]{0:T(1024)S(1)} %add_rsqrt_fusion, f32[2048]{0:T(1024)S(1)} %copy-done.17), kind=kOutput, calls=%fused_computation.27 | convolution fusion | flops 2224078848 | bytes 10267648 | tf_op jit(solution)/shard_map/dot_general | solution.py:164
  415.7 29.9 %reduce-scatter.3.cloned.1.call-done = bf16[768,512]{1,0:T(8,128)(2,1)} async-done(((bf16[768,2048]{1,0:T(8,128)(2,1)}), bf16[768,512]{1,0:T(8,128)(2,1)}) %reduce-scatter.3.cloned.1.call-update) | async-done | bytes 786448 | tf_op jit(solution)/shard_map/reduce_scatter | solution.py:167
  445.6 2.1 reshape.274
  447.8 10.9 %all-to-all-start.3 = ((bf16[64,12,512]{2,1,0:T(8,128)(2,1)}), bf16[64,12,512]{2,1,0:T(8,128)(2,1)S(1)}, u32[]{:S(2)}, u32[]{:S(2)}) async-start(bf16[64,12,512]{2,1,0:T(8,128)(2,1)} %reshape.274), calls=%async_computation.4 | async-start | bytes 2097152 | tf_op jit(solution)/shard_map/all_to_all | solution.py:170
  458.6 30.0 %reduce-scatter.5.cloned.1.call-done = bf16[768,512]{1,0:T(8,128)(2,1)} async-done(((bf16[768,2048]{1,0:T(8,128)(2,1)}), bf16[768,512]{1,0:T(8,128)(2,1)}) %reduce-scatter.5.cloned.1.call-update) | async-done | bytes 786448 | tf_op jit(solution)/shard_map/reduce_scatter | solution.py:167
  488.7 2.2 reshape.276
  490.8 10.9 %all-to-all-start.5 = ((bf16[64,12,512]{2,1,0:T(8,128)(2,1)}), bf16[64,12,512]{2,1,0:T(8,128)(2,1)}, u32[]{:S(2)}, u32[]{:S(2)}) async-start(bf16[64,12,512]{2,1,0:T(8,128)(2,1)} %reshape.276), calls=%async_computation.7 | async-start | bytes 2097152 | tf_op jit(solution)/shard_map/all_to_all | solution.py:170
  501.8 0.1 mul.276
  502.0 28.2 %all-to-all-done.5 = bf16[64,12,512]{2,1,0:T(8,128)(2,1)} async-done(((bf16[64,12,512]{2,1,0:T(8,128)(2,1)}), bf16[64,12,512]{2,1,0:T(8,128)(2,1)}, u32[]{:S(2)}, u32[]{:S(2)}) %all-to-all-start.5) | async-done | bytes 786464 | tf_op jit(solution)/shard_map/all_to_all | solution.py:170
  530.2 1.7 pad_maximum_fusion
  531.9 2.7 gather_fusion
  534.6 0.3 reshape.278
  534.9 1.1 fusion.93
  536.0 1.1 fusion.67
  537.2 11.7 %all_to_all.41 = bf16[4,128,512]{2,1,0:T(8,128)(2,1)S(1)} all-to-all(bf16[4,128,512]{2,1,0:T(8,128)(2,1)S(1)} %broadcast_in_dim.20), channel_id=1, replica_groups=mesh['seq'=64,'tp'=4] {'tp'}, dimensions={0} | all-to-all | bytes 1048576 | tf_op jit(solution)/shard_map/all_to_all | solution.py:183
  548.9 0.3 copy.116
  549.2 1.0 copy.117
  (69 shorter events, 1.4 us)
Async XLA Ops:
  7.2 1.8 copy-start
  7.2 3.9 copy-start.14
  11.2 5.9 %copy-start.10 = (bf16[128,576]{0,1:T(8,128)(2,1)}, bf16[128,576]{0,1:T(8,128)(2,1)S(1)}, u32[]{:S(2)}) copy-start(bf16[128,576]{0,1:T(8,128)(2,1)S(1)} %pad_maximum_fusion.1) | copy-start | bytes 442372
  17.2 13.5 %copy-start.12 = (s32[128,6]{0,1:T(8,128)S(1)}, s32[128,6]{0,1:T(8,128)}, u32[]{:S(2)}) copy-start(s32[128,6]{0,1:T(8,128)} %param.21) | copy-start | bytes 9220
  17.2 13.9 %copy-start.3 = (bf16[128,2048]{1,0:T(8,128)(2,1)S(1)}, bf16[128,2048]{1,0:T(8,128)(2,1)}, u32[]{:S(2)}) copy-start(bf16[128,2048]{1,0:T(8,128)(2,1)} %param.13) | copy-start | bytes 1572868
  17.2 13.9 %copy-start.8 = (bf16[2048,384]{1,0:T(8,128)(2,1)S(1)}, bf16[2048,384]{1,0:T(8,128)(2,1)}, u32[]{:S(2)}) copy-start(bf16[2048,384]{1,0:T(8,128)(2,1)} %param.15) | copy-start | bytes 4718596
  17.2 221.7 %all-to-all-start = ((bf16[64,128,576]{1,2,0:T(8,128)(2,1)}), bf16[64,128,576]{1,2,0:T(8,128)(2,1)}, u32[]{:S(2)}, u32[]{:S(2)}) async-start(bf16[64,128,576]{1,2,0:T(8,128)(2,1)} %tile.2), calls=%async_computation | async-start | bytes 18874368 | tf_op jit(solution)/shard_map/all_to_all | solution.py:91
  30.6 1.7 copy-start.11
  245.6 3.4 copy-start.2
  260.4 9.2 %copy-start.9 = (bf16[256,2048]{1,0:T(8,128)(2,1)S(1)}, bf16[256,2048]{1,0:T(8,128)(2,1)}, u32[]{:S(2)}) copy-start(bf16[256,2048]{1,0:T(8,128)(2,1)} %param.19) | copy-start | bytes 3145732
  270.8 13.9 %all-to-all-start.1 = ((bf16[4,128,512]{2,1,0:T(8,128)(2,1)}), bf16[4,128,512]{2,1,0:T(8,128)(2,1)S(1)}, u32[]{:S(2)}, u32[]{:S(2)}) async-start(bf16[4,128,512]{2,1,0:T(8,128)(2,1)} %bitcast.130), calls=%async_computation.1 | async-start | bytes 1048576 | tf_op jit(solution)/shard_map/all_to_all | solution.py:123
  274.8 83.0 %all-gather.3.cloned.1.call-start = ((), (), s32[]{:S(2)}) async-start(), calls=%async_computation.9 | async-start | bytes 3932160 | tf_op jit(solution)/shard_map/all_gather | solution.py:155
  284.8 1.1 copy-start.6
  320.8 81.1 %all-gather.5.cloned.1.call-start = ((), (), s32[]{:S(2)}) async-start(), calls=%async_computation.11 | async-start | bytes 3932160 | tf_op jit(solution)/shard_map/all_gather | solution.py:155
  355.4 5.2 copy-start.17
  356.5 89.2 %reduce-scatter.3.cloned.1.call-start = ((), (), s32[]{:S(2)}) async-start(), calls=%async_computation.10 | async-start | bytes 3932160 | tf_op jit(solution)/shard_map/reduce_scatter | solution.py:167
  357.8 2.8 copy-start.5
  360.7 3.9 copy-start.16
  372.7 32.0 %copy-start.15 = (bf16[1,2048,352]{1,2,0:T(8,128)(2,1)S(1)}, bf16[1,2048,352]{1,2,0:T(8,128)(2,1)}, u32[]{:S(2)}) copy-start(bf16[1,2048,352]{1,2,0:T(8,128)(2,1)} %param.23) | copy-start | bytes 4325380
  372.7 115.9 %reduce-scatter.5.cloned.1.call-start = ((), (), s32[]{:S(2)}) async-start(), calls=%async_computation.12 | async-start | bytes 3932160 | tf_op jit(solution)/shard_map/reduce_scatter | solution.py:167
  401.9 2.8 copy-start.4
  447.8 54.2 %copy-start.13 = (f32[128,6]{0,1:T(8,128)S(1)}, f32[128,6]{0,1:T(8,128)}, u32[]{:S(2)}) copy-start(f32[128,6]{0,1:T(8,128)} %param.22) | copy-start | bytes 9220
  447.8 43.1 %all-to-all-start.3 = ((bf16[64,12,512]{2,1,0:T(8,128)(2,1)}), bf16[64,12,512]{2,1,0:T(8,128)(2,1)S(1)}, u32[]{:S(2)}, u32[]{:S(2)}) async-start(bf16[64,12,512]{2,1,0:T(8,128)(2,1)} %reshape.274), calls=%async_computation.4 | async-start | bytes 2097152 | tf_op jit(solution)/shard_map/all_to_all | solution.py:170
  490.8 39.4 %all-to-all-start.5 = ((bf16[64,12,512]{2,1,0:T(8,128)(2,1)}), bf16[64,12,512]{2,1,0:T(8,128)(2,1)}, u32[]{:S(2)}, u32[]{:S(2)}) async-start(bf16[64,12,512]{2,1,0:T(8,128)(2,1)} %reshape.276), calls=%async_computation.7 | async-start | bytes 2097152 | tf_op jit(solution)/shard_map/all_to_all | solution.py:170
  534.9 1.2 copy-start.7
  534.9 15.3 %copy-start.1 = (bf16[2048,576]{0,1:T(8,128)(2,1)S(1)}, bf16[2048,576]{0,1:T(8,128)(2,1)}, u32[]{:S(2)}) copy-start(bf16[2048,576]{0,1:T(8,128)(2,1)} %param.16) | copy-start | bytes 7077892
Sparse Core Ops, SparseCore 0:
  321.0 36.8 all-gather.2
  359.6 42.2 all-gather.4
  404.5 41.1 reduce-scatter.2
  448.0 40.5 reduce-scatter.4
